TPU v7x, 512 devices: a whole 4x4x16 slice. The times are simulated.
512 devices in a mesh: freq: 32 (over z_lo, x), src: 2 (over z_hi), rcv: 8 (over y, core).
Axes of the slice: x: 4, y: 4, z: 16 (z_hi: 2, z_lo: 8; z = z_hi * 8 + z_lo), core: 2. Of those that a mesh axis runs over, the one named last changes fastest.
Arguments:
- traces: float32 [1024, 1024, 256], P(('src', 'freq'), 'rcv'), may hold values from -6 to 6
Outputs:
- multiples: float32 [2, 96, 1024, 1024], P(None, 'freq', 'src', 'rcv')
All inputs are finite; a program needn't handle non-finite values.
Results may differ from a plain program's by a relative error of at most 0.000098.
Values sent between devices are 32-bit elements; how exact they have to be, the bound alone decides.
A program may use at most 64 MiB of HBM per device.

v0:
```python
import math
import jax
import jax.numpy as jnp
from jax import lax
from jax.sharding import PartitionSpec as P

N = 1024
FPD = 3


def dft_matrix(n_time, n_freq):
    times = jnp.arange(n_time, dtype=jnp.int32)
    bins = jnp.arange(n_freq, dtype=jnp.int32)
    phase = times[:, None] * bins[None, :] % n_time
    angle = phase.astype(jnp.float32) * (2.0 * math.pi / n_time)
    both = jnp.stack([jnp.cos(angle), -jnp.sin(angle)], axis=-1)
    return both.reshape(n_time, 2 * n_freq) * (1.0 / math.sqrt(n_time))


def batched_dot(left, right):
    return jnp.einsum(
        "mgq,mqn->mgn",
        left,
        right,
        precision=lax.Precision.HIGHEST,
        preferred_element_type=jnp.float32,
    )


def complex_product(left_re, left_im, right_re, right_im):
    real_part = batched_dot(left_re, right_re) - batched_dot(left_im, right_im)
    imag_part = batched_dot(left_re, right_im) + batched_dot(left_im, right_re)
    return (real_part, imag_part)


def per_device(traces):
    n_time = traces.shape[2]
    n_freq = FPD * lax.axis_size("freq")
    dft_table = dft_matrix(n_time, n_freq)
    spectra = jnp.einsum(
        "srt,tk->ksr",
        traces,
        dft_table,
        precision=lax.Precision.HIGHEST,
        preferred_element_type=jnp.float32,
    )
    regrouped = lax.all_to_all(spectra, "freq", split_axis=0, concat_axis=1, tiled=True)
    src_rows = regrouped.shape[1]
    rcv_cols = regrouped.shape[2]
    split_parts = regrouped.reshape(FPD, 2, src_rows, rcv_cols)
    local_re = split_parts[:, 0]
    local_im = split_parts[:, 1]
    col_re, col_im = (
        lax.all_gather(local_re, "src", axis=1, tiled=True),
        lax.all_gather(local_im, "src", axis=1, tiled=True),
    )
    piece_re = lax.all_gather(local_re, "rcv", axis=2, tiled=True)
    piece_im = lax.all_gather(local_im, "rcv", axis=2, tiled=True)
    real_part, imag_part = complex_product(piece_re, piece_im, col_re, col_im)
    scale = -1.0 / math.sqrt(N)
    return jnp.stack([real_part, imag_part]) * scale


def solution(mesh):
    in_specs = (P(("src", "freq"), "rcv", None),)
    out_specs = P(None, "freq", "src", "rcv")
    return jax.shard_map(
        per_device, mesh=mesh, in_specs=in_specs, out_specs=out_specs, check_vma=False
    )
```

profile of v0, /device:TPU:1, one launch (start us, length us, event | category | flops | bytes accessed | tf_op | source)
XLA Modules:
  0.0 411.7 jit_solution(3908307167513742405)
XLA Ops:
  6.5 0.0 copy-start
  6.5 0.0 all-gather.11.cloned.1.call-start
  6.5 0.4 sine_negate_fusion
  7.0 0.2 copy.14
  7.1 0.1 reshape.83
  7.3 0.8 copy-done
  8.1 2.3 fusion.39
  10.4 0.9 copy.15
  11.3 89.4 %all_to_all.15 = f32[192,16,128]{2,1,0:T(8,128)S(1)} all-to-all(f32[192,16,128]{2,1,0:T(8,128)S(1)} %copy.15), channel_id=1, replica_groups=mesh['freq'=32,'src'=2,'rcv'=8] {'freq'}, dimensions={0} | all-to-all | bytes 3145728 | tf_op jit(solution)/shard_map/all_to_all | solution.py:47
  100.7 0.1 copy.16
  100.9 1.3 slice_bitcast_fusion.1
  102.1 0.0 all-gather.11.cloned.1.call-update
  102.1 0.0 all-gather.13.cloned.1.call-start
  102.2 0.7 all-gather.13.cloned.1.call-update
  102.9 0.0 all-gather.15.cloned.1.call-start
  102.9 0.7 all-gather.15.cloned.1.call-update
  103.6 0.2 all-gather.9.cloned.1.call-start
  103.9 0.3 all-gather.9.cloned.1.call-update
  104.2 90.4 %all-gather.11.cloned.1.call-done = f32[3,1,1024,128]{3,2,0,1:T(8,128)} async-done(((f32[3,1,512,128]{3,2,0,1:T(8,128)}), f32[3,1,1024,128]{3,2,0,1:T(8,128)}) %all-gather.11.cloned.1.call-update) | async-done | bytes 1572880 | tf_op jit(solution)/shard_map/all_gather | solution.py:54
  194.6 48.8 %all-gather.13.cloned.1.call-done = f32[3,1,512,1024]{3,2,0,1:T(8,128)} async-done(((f32[3,1,512,128]{3,2,0,1:T(8,128)}), f32[3,1,512,1024]{3,2,0,1:T(8,128)}) %all-gather.13.cloned.1.call-update) | async-done | bytes 6291472 | tf_op jit(solution)/shard_map/all_gather | solution.py:58
  243.4 7.9 %fusion = f32[3,512,128]{2,1,0:T(8,128)S(1)} fusion(f32[3,1,512,1024]{3,2,0,1:T(8,128)} %all-gather.13.cloned.1.call-done, f32[3,1,1024,128]{3,2,0,1:T(8,128)} %all-gather.11.cloned.1.call-done), kind=kOutput, calls=%fused_computation | convolution fusion | flops 2415919104 | bytes 8650752 | tf_op jit(solution)/shard_map/mgq,mqn->mgn/dot_general | solution.py:21
  251.3 90.1 %all-gather.15.cloned.1.call-done = f32[3,1,1024,128]{3,2,0,1:T(8,128)} async-done(((f32[3,1,512,128]{3,2,0,1:T(8,128)}), f32[3,1,1024,128]{3,2,0,1:T(8,128)}) %all-gather.15.cloned.1.call-update) | async-done | bytes 1572880 | tf_op jit(solution)/shard_map/all_gather | solution.py:55
  341.4 8.8 %fusion.2 = f32[3,512,128]{2,1,0:T(8,128)} fusion(f32[3,1,512,1024]{3,2,0,1:T(8,128)} %all-gather.13.cloned.1.call-done, f32[3,1,1024,128]{3,2,0,1:T(8,128)} %all-gather.15.cloned.1.call-done), kind=kOutput, calls=%fused_computation.2 | convolution fusion | flops 2415919104 | bytes 8650752 | tf_op jit(solution)/shard_map/mgq,mqn->mgn/dot_general | solution.py:21
  350.2 39.8 %all-gather.9.cloned.1.call-done = f32[3,1,512,1024]{3,2,0,1:T(8,128)} async-done(((f32[3,1,512,128]{3,2,0,1:T(8,128)}), f32[3,1,512,1024]{3,2,0,1:T(8,128)}) %all-gather.9.cloned.1.call-update) | async-done | bytes 6291472 | tf_op jit(solution)/shard_map/all_gather | solution.py:57
  390.1 0.0 copy-start.1
  390.1 0.0 copy-start.2
  390.1 0.0 copy-start.3
  390.1 8.4 %fusion.22 = f32[1,3,512,128]{3,2,1,0:T(8,128)S(1)} fusion(f32[3,512,128]{2,1,0:T(8,128)S(1)} %fusion, f32[3,1,1024,128]{3,2,0,1:T(8,128)} %all-gather.15.cloned.1.call-done, f32[3,1,512,1024]{3,2,0,1:T(8,128)} %all-gather.9.cloned.1.call-done), kind=kOutput, calls=%fused_computation.15 | convolution fusion | flops 2416115712 | bytes 9437184 | tf_op jit(solution)/shard_map/mgq,mqn->mgn/dot_general | solution.py:21
  398.5 0.0 copy-done.1
  398.5 0.0 copy-done.2
  398.5 0.0 copy-done.3
  398.5 5.4 %fusion.27 = f32[1,3,512,128]{3,2,1,0:T(8,128)S(1)} fusion(f32[3,512,128]{2,1,0:T(8,128)S(1)} %copy-done.3, f32[3,1,1024,128]{3,2,0,1:T(8,128)S(1)} %copy-done.2, f32[3,1,512,1024]{3,2,0,1:T(8,128)S(1)} %copy-done.1), kind=kOutput, calls=%fused_computation.16 | convolution fusion | flops 2416115712 | bytes 9437184 | tf_op jit(solution)/shard_map/mgq,mqn->mgn/dot_general | solution.py:21
  403.9 1.2 maximum_multiply_fusion
  (1 shorter events, 0.0 us)
Async XLA Ops:
  6.5 1.6 copy-start
  6.5 188.0 %all-gather.11.cloned.1.call-start = ((), (), s32[]{:S(2)}) async-start(), calls=%async_computation.2 | async-start | bytes 2359296 | tf_op jit(solution)/shard_map/all_gather | solution.py:54
  102.1 141.2 %all-gather.13.cloned.1.call-start = ((), (), s32[]{:S(2)}) async-start(), calls=%async_computation.3 | async-start | bytes 7077888 | tf_op jit(solution)/shard_map/all_gather | solution.py:58
  102.9 238.5 %all-gather.15.cloned.1.call-start = ((), (), s32[]{:S(2)}) async-start(), calls=%async_computation.4 | async-start | bytes 2359296 | tf_op jit(solution)/shard_map/all_gather | solution.py:55
  103.6 286.5 %all-gather.9.cloned.1.call-start = ((), (), s32[]{:S(2)}) async-start(), calls=%async_computation.1 | async-start | bytes 7077888 | tf_op jit(solution)/shard_map/all_gather | solution.py:57
  390.1 8.4 %copy-start.1 = (f32[3,1,512,1024]{3,2,0,1:T(8,128)S(1)}, f32[3,1,512,1024]{3,2,0,1:T(8,128)}, u32[]{:S(2)}) copy-start(f32[3,1,512,1024]{3,2,0,1:T(8,128)} %all-gather.9.cloned.1.call-done) | copy-start | bytes 18874372
  390.1 8.4 %copy-start.2 = (f32[3,1,1024,128]{3,2,0,1:T(8,128)S(1)}, f32[3,1,1024,128]{3,2,0,1:T(8,128)}, u32[]{:S(2)}) copy-start(f32[3,1,1024,128]{3,2,0,1:T(8,128)} %all-gather.11.cloned.1.call-done) | copy-start | bytes 4718596
  390.1 8.4 %copy-start.3 = (f32[3,512,128]{2,1,0:T(8,128)S(1)}, f32[3,512,128]{2,1,0:T(8,128)}, u32[]{:S(2)}) copy-start(f32[3,512,128]{2,1,0:T(8,128)} %fusion.2) | copy-start | bytes 2359300
Sparse Core Ops, SparseCore 0:
  102.3 92.2 all-gather.10
  196.7 46.6 all-gather.12
  245.5 95.8 all-gather.14
  343.4 46.6 all-gather.8
where the time goes:
time: 412 us
  waiting for transfers between devices  271 us (66%)
  blocking collectives  89.4 us (22%)
  matrix products  32.8 us (8%)
  between operations  13.2 us (3%)
    all_gather x1, waiting for transfers between devices, per_device(): lax.all_gather(local_re, 'src', axis=1, tiled=True)  90.4 us
    all_gather x1, waiting for transfers between devices, per_device(): lax.all_gather(local_im, 'src', axis=1, tiled=True)  90.1 us
    all_to_all x1, blocking collectives, per_device(): lax.all_to_all(spectra, 'freq', split_axis=0, concat_axis=1, tiled=True)  89.4 us
    all_gather x1, waiting for transfers between devices, per_device(): piece_im = lax.all_gather(local_im, 'rcv', axis=2, tiled=True)  48.8 us
    all_gather x1, waiting for transfers between devices, per_device(): piece_re = lax.all_gather(local_re, 'rcv', axis=2, tiled=True)  39.8 us
    dot_general x4, matrix products, batched_dot(): jnp.einsum('mgq,mqn->mgn', left, right, precision=lax.Precision.HIGHEST,...  30.5 us
  transfers between devices with their start and end apart: 4, of which 4 were waited for; matrix products, arithmetic and copies ran while one was open for 4% of the time, Pallas kernels for 0%

commit v1 on v0

--- a/solution.py
+++ b/solution.py
@@ -44,7 +44,15 @@
         precision=lax.Precision.HIGHEST,
         preferred_element_type=jnp.float32,
     )
-    regrouped = lax.all_to_all(spectra, "freq", split_axis=0, concat_axis=1, tiled=True)
+    regrouped = jnp.concatenate(
+        lax.all_to_all(
+            jnp.stack(jnp.split(spectra, lax.axis_size("freq"), axis=0)),
+            axis_name="freq",
+            split_axis=0,
+            concat_axis=0,
+        ),
+        axis=1,
+    )
     src_rows = regrouped.shape[1]
     rcv_cols = regrouped.shape[2]
     split_parts = regrouped.reshape(FPD, 2, src_rows, rcv_cols)

time: 412 us -> 412 us (level)
  no operation moved by 1% of the time
where the time goes in v1:
time: 412 us
  waiting for transfers between devices  271 us (66%)
  blocking collectives  89.4 us (22%)
  matrix products  32.8 us (8%)
  between operations  13.5 us (3%)
    all_gather x1, waiting for transfers between devices, per_device(): lax.all_gather(local_re, 'src', axis=1, tiled=True)  90.4 us
    all_gather x1, waiting for transfers between devices, per_device(): lax.all_gather(local_im, 'src', axis=1, tiled=True)  90.1 us
    all_to_all x1, blocking collectives, per_device(): lax.all_to_all(jnp.stack(jnp.split(spectra, lax.axis_size('freq'), axis=0...  89.4 us
    all_gather x1, waiting for transfers between devices, per_device(): piece_im = lax.all_gather(local_im, 'rcv', axis=2, tiled=True)  48.8 us
    all_gather x1, waiting for transfers between devices, per_device(): piece_re = lax.all_gather(local_re, 'rcv', axis=2, tiled=True)  39.8 us
    dot_general x4, matrix products, batched_dot(): jnp.einsum('mgq,mqn->mgn', left, right, precision=lax.Precision.HIGHEST,...  30.5 us
  transfers between devices with their start and end apart: 4, of which 4 were waited for; matrix products, arithmetic and copies ran while one was open for 4% of the time, Pallas kernels for 0%

profile of v1, /device:TPU:1, one launch (start us, length us, event | category | flops | bytes accessed | tf_op | source)
XLA Modules:
  0.0 411.7 jit_solution(864384014348216134)
XLA Ops:
  6.5 0.0 copy-start
  6.5 0.0 all-gather.11.cloned.1.call-start
  6.5 0.4 sine_negate_fusion
  7.0 0.2 copy.15
  7.1 0.1 reshape.82
  7.3 0.8 copy-done
  8.1 2.3 fusion.39
  11.1 0.3 copy.16
  11.4 89.4 %all_to_all.5 = f32[32,6,16,128]{3,2,1,0:T(8,128)S(1)} all-to-all(f32[32,6,16,128]{3,2,1,0:T(8,128)S(1)} %copy.16), channel_id=1, replica_groups=mesh['freq'=32,'src'=2,'rcv'=8] {'freq'}, dimensions={0} | all-to-all | bytes 3145728 | tf_op jit(solution)/shard_map/all_to_all | solution.py:48
  100.7 0.1 copy.17
  100.9 1.3 slice_bitcast_fusion.1
  102.1 0.0 all-gather.11.cloned.1.call-update
  102.1 0.0 all-gather.13.cloned.1.call-start
  102.2 0.7 all-gather.13.cloned.1.call-update
  102.9 0.0 all-gather.15.cloned.1.call-start
  102.9 0.7 all-gather.15.cloned.1.call-update
  103.6 0.2 all-gather.9.cloned.1.call-start
  103.9 0.3 all-gather.9.cloned.1.call-update
  104.2 90.4 %all-gather.11.cloned.1.call-done = f32[3,1,1024,128]{3,2,0,1:T(8,128)} async-done(((f32[3,1,512,128]{3,2,0,1:T(8,128)}), f32[3,1,1024,128]{3,2,0,1:T(8,128)}) %all-gather.11.cloned.1.call-update) | async-done | bytes 1572880 | tf_op jit(solution)/shard_map/all_gather | solution.py:62
  194.6 48.8 %all-gather.13.cloned.1.call-done = f32[3,1,512,1024]{3,2,0,1:T(8,128)} async-done(((f32[3,1,512,128]{3,2,0,1:T(8,128)}), f32[3,1,512,1024]{3,2,0,1:T(8,128)}) %all-gather.13.cloned.1.call-update) | async-done | bytes 6291472 | tf_op jit(solution)/shard_map/all_gather | solution.py:66
  243.4 7.9 %fusion = f32[3,512,128]{2,1,0:T(8,128)S(1)} fusion(f32[3,1,512,1024]{3,2,0,1:T(8,128)} %all-gather.13.cloned.1.call-done, f32[3,1,1024,128]{3,2,0,1:T(8,128)} %all-gather.11.cloned.1.call-done), kind=kOutput, calls=%fused_computation | convolution fusion | flops 2415919104 | bytes 8650752 | tf_op jit(solution)/shard_map/mgq,mqn->mgn/dot_general | solution.py:21
  251.4 90.1 %all-gather.15.cloned.1.call-done = f32[3,1,1024,128]{3,2,0,1:T(8,128)} async-done(((f32[3,1,512,128]{3,2,0,1:T(8,128)}), f32[3,1,1024,128]{3,2,0,1:T(8,128)}) %all-gather.15.cloned.1.call-update) | async-done | bytes 1572880 | tf_op jit(solution)/shard_map/all_gather | solution.py:63
  341.4 8.8 %fusion.2 = f32[3,512,128]{2,1,0:T(8,128)} fusion(f32[3,1,512,1024]{3,2,0,1:T(8,128)} %all-gather.13.cloned.1.call-done, f32[3,1,1024,128]{3,2,0,1:T(8,128)} %all-gather.15.cloned.1.call-done), kind=kOutput, calls=%fused_computation.2 | convolution fusion | flops 2415919104 | bytes 8650752 | tf_op jit(solution)/shard_map/mgq,mqn->mgn/dot_general | solution.py:21
  350.2 39.8 %all-gather.9.cloned.1.call-done = f32[3,1,512,1024]{3,2,0,1:T(8,128)} async-done(((f32[3,1,512,128]{3,2,0,1:T(8,128)}), f32[3,1,512,1024]{3,2,0,1:T(8,128)}) %all-gather.9.cloned.1.call-update) | async-done | bytes 6291472 | tf_op jit(solution)/shard_map/all_gather | solution.py:65
  390.1 0.0 copy-start.1
  390.1 0.0 copy-start.2
  390.1 0.0 copy-start.3
  390.1 8.4 %fusion.22 = f32[1,3,512,128]{3,2,1,0:T(8,128)S(1)} fusion(f32[3,512,128]{2,1,0:T(8,128)S(1)} %fusion, f32[3,1,1024,128]{3,2,0,1:T(8,128)} %all-gather.15.cloned.1.call-done, f32[3,1,512,1024]{3,2,0,1:T(8,128)} %all-gather.9.cloned.1.call-done), kind=kOutput, calls=%fused_computation.15 | convolution fusion | flops 2416115712 | bytes 9437184 | tf_op jit(solution)/shard_map/mgq,mqn->mgn/dot_general | solution.py:21
  398.5 0.0 copy-done.1
  398.5 0.0 copy-done.2
  398.5 0.0 copy-done.3
  398.5 5.4 %fusion.27 = f32[1,3,512,128]{3,2,1,0:T(8,128)S(1)} fusion(f32[3,512,128]{2,1,0:T(8,128)S(1)} %copy-done.3, f32[3,1,1024,128]{3,2,0,1:T(8,128)S(1)} %copy-done.2, f32[3,1,512,1024]{3,2,0,1:T(8,128)S(1)} %copy-done.1), kind=kOutput, calls=%fused_computation.16 | convolution fusion | flops 2416115712 | bytes 9437184 | tf_op jit(solution)/shard_map/mgq,mqn->mgn/dot_general | solution.py:21
  403.9 1.2 maximum_multiply_fusion
  (33 shorter events, 0.4 us)
Async XLA Ops:
  6.5 1.6 copy-start
  6.5 188.0 %all-gather.11.cloned.1.call-start = ((), (), s32[]{:S(2)}) async-start(), calls=%async_computation.2 | async-start | bytes 2359296 | tf_op jit(solution)/shard_map/all_gather | solution.py:62
  102.1 141.2 %all-gather.13.cloned.1.call-start = ((), (), s32[]{:S(2)}) async-start(), calls=%async_computation.3 | async-start | bytes 7077888 | tf_op jit(solution)/shard_map/all_gather | solution.py:66
  102.9 238.5 %all-gather.15.cloned.1.call-start = ((), (), s32[]{:S(2)}) async-start(), calls=%async_computation.4 | async-start | bytes 2359296 | tf_op jit(solution)/shard_map/all_gather | solution.py:63
  103.6 286.5 %all-gather.9.cloned.1.call-start = ((), (), s32[]{:S(2)}) async-start(), calls=%async_computation.1 | async-start | bytes 7077888 | tf_op jit(solution)/shard_map/all_gather | solution.py:65
  390.1 8.4 %copy-start.1 = (f32[3,1,512,1024]{3,2,0,1:T(8,128)S(1)}, f32[3,1,512,1024]{3,2,0,1:T(8,128)}, u32[]{:S(2)}) copy-start(f32[3,1,512,1024]{3,2,0,1:T(8,128)} %all-gather.9.cloned.1.call-done) | copy-start | bytes 18874372
  390.1 8.4 %copy-start.2 = (f32[3,1,1024,128]{3,2,0,1:T(8,128)S(1)}, f32[3,1,1024,128]{3,2,0,1:T(8,128)}, u32[]{:S(2)}) copy-start(f32[3,1,1024,128]{3,2,0,1:T(8,128)} %all-gather.11.cloned.1.call-done) | copy-start | bytes 4718596
  390.1 8.4 %copy-start.3 = (f32[3,512,128]{2,1,0:T(8,128)S(1)}, f32[3,512,128]{2,1,0:T(8,128)}, u32[]{:S(2)}) copy-start(f32[3,512,128]{2,1,0:T(8,128)} %fusion.2) | copy-start | bytes 2359300
Sparse Core Ops, SparseCore 0:
  102.3 92.2 all-gather.10
  196.7 46.6 all-gather.12
  245.5 95.8 all-gather.14
  343.4 46.6 all-gather.8
